TPU v7x, 32 devices: a whole 2x2x4 slice. The times are simulated.
32 devices in a mesh: pb: 4 (over y, core), kv: 8 (over z, x).
Axes of the slice: x: 2, y: 2, z: 4, core: 2. Of those that a mesh axis runs over, the one named last changes fastest.
Arguments:
- queries: bfloat16 [8192, 128], P(('pb', 'kv')), may hold values from -15 to 15
- query_tangent: bfloat16 [8192, 128], P(('pb', 'kv')), may hold values from -2 to 2
- keys: bfloat16 [8192, 128], P(('pb', 'kv')), may hold values from -8 to 8
- values: bfloat16 [8192, 128], P(('pb', 'kv')), may hold values from -6 to 6
- key_tangent: bfloat16 [8192, 128], P(('pb', 'kv')), may hold values from -2 to 2
- value_tangent: bfloat16 [8192, 128], P(('pb', 'kv')), may hold values from -6 to 6
- block_list: int32 [64, 8, 8], P('pb', 'kv'), may hold values from 0 to 63, as said below
- block_count: int32 [64, 8], P('pb', 'kv'), may hold values from 1 to 8, as said below
Outputs:
- attended: bfloat16 [8192, 128], P(('pb', 'kv'))
- attended_tangent: bfloat16 [8192, 128], P(('pb', 'kv'))
Inputs may be any that keep to these rules, and one draw needn't show every extreme that they name: `block_list`: entries for one query block and slab j are distinct key blocks g whose index g // (256 // 128) leaves remainder j when divided by 8; entries past block_count are valid but unused. `block_count`: the value 8 is reached in every key slab.
All inputs are finite; a program needn't handle non-finite values.
Results may differ from a plain program's by a relative error of at most 0.01.
Values may be sent and summed in bfloat16 or wider, within the bound.
A program may use at most 128 MiB of HBM per device.

v0:
```python
import functools
import math

import jax
import jax.numpy as jnp
from jax import lax
from jax.experimental import pallas as pl
from jax.experimental.pallas import tpu as pltpu
from jax.sharding import PartitionSpec as P

BLK = 128
NT = (((1,), (1,)), ((), ()))
MESH = pl.DeviceIdType.MESH


def flip(a, b, bits):
    out = 0
    for k in range(bits):
        w = 1 << k
        out = out + (a // w + b // w) % 2 * w
    return out


def kernel(
    zc, slabs, q_in, qt_in, k_in, v_in, kt_in, vt_in, list_in, count_in, out_ref,
    kv, qq, lst, cnt, bias, s_scr, p_scr, ps_scr, send, sstat, recv, rstat, coef,
    local_sem, ks, kr, qs, qr, bs, rs, rr, ts, tr,
):
    rows, hd = q_in.shape
    half = rows // 2
    bits = zc.bit_length() - 1
    scale = 1.0 / math.sqrt(hd)
    factor = scale * math.log2(math.e)
    pb, kvi = lax.axis_index("pb"), lax.axis_index("kv")
    y, c, z, x = pb // 2, pb % 2, kvi // 2, kvi % 2
    to_x = (pb, kvi + 1 - 2 * x)
    to_y = (pb + 2 - 4 * y, kvi)
    to_c = (pb + 1 - 2 * c, kvi)

    def to_z(mask):
        return (pb, flip(z, mask, bits) * 2 + x)

    loads = []
    for n, (src, dst) in enumerate(
        [
            (k_in, kv.at[0, :, pl.ds(0, hd)]),
            (kt_in, kv.at[0, :, pl.ds(hd, hd)]),
            (v_in, kv.at[0, :, pl.ds(2 * hd, hd)]),
            (vt_in, kv.at[0, :, pl.ds(3 * hd, hd)]),
            (qt_in, qq.at[0, :, pl.ds(0, hd)]),
            (q_in, qq.at[0, :, pl.ds(hd, hd)]),
            (list_in, lst.at[0]),
            (count_in, cnt.at[0]),
        ]
    ):
        copy = pltpu.make_async_copy(src, dst, local_sem.at[n])
        copy.start()
        loads.append(copy)

    barrier = pltpu.get_barrier_semaphore()
    for dev in [to_x, to_y, to_c] + [to_z(m) for m in range(1, zc)]:
        pl.semaphore_signal(barrier, inc=1, device_id=dev, device_id_type=MESH)
    pl.semaphore_wait(barrier, 2 + zc)
    for copy in loads:
        copy.wait()

    def remote(src, dst, ssem, rsem, dev):
        return pltpu.make_async_remote_copy(
            src_ref=src, dst_ref=dst, send_sem=ssem, recv_sem=rsem,
            device_id=dev, device_id_type=MESH,
        )

    sent = []

    def piece(slot, h):
        return kv.at[slot, pl.ds(h * half, half)]

    def give(slot, h, dst, dev):
        copy = remote(piece(slot, h), piece(dst, h), ks.at[dst, h], kr.at[dst, h], dev)
        copy.start()
        sent.append(copy)

    def got(slot, h):
        remote(piece(slot, h), piece(slot, h), ks.at[slot, h], kr.at[slot, h], to_c).wait_recv()

    give(0, 1, 1, to_x)
    give(0, 0, 2, to_y)
    give(0, 0, 1, to_x)
    give(0, 1, 2, to_y)
    for m in range(zc - 1, 0, -1):
        copy = remote(qq.at[0], qq.at[m], qs.at[m], qr.at[m], to_z(m))
        copy.start()
        sent.append(copy)
    give(0, 0, 4, to_c)
    give(0, 1, 4, to_c)
    tables = [
        remote(lst.at[0], lst.at[1], bs.at[0], bs.at[1], to_x),
        remote(cnt.at[0], cnt.at[1], bs.at[2], bs.at[3], to_x),
    ]
    for copy in tables:
        copy.start()

    def mask_rows(side):
        blocks = lst.shape[2]
        shard_blocks = rows // BLK
        slab_blocks = 4 * shard_blocks
        ids = lst[side]
        local = ids // (shard_blocks * slabs) * shard_blocks + ids % shard_blocks
        used = lax.broadcasted_iota(jnp.int32, ids.shape, 0) < cnt[side]
        row = lax.broadcasted_iota(jnp.int32, (slab_blocks, blocks), 0)
        on = jnp.zeros((slab_blocks, blocks), jnp.float32)
        for g in range(slab_blocks):
            hit = jnp.max(jnp.where((local == g) & used, 1.0, 0.0), axis=0, keepdims=True)
            on = jnp.where(row == g, hit, on)
        spread = jnp.where(
            lax.broadcasted_iota(jnp.int32, (slab_blocks, 4 * rows), 1) // BLK
            == lax.broadcasted_iota(jnp.int32, (slab_blocks, 4 * rows), 0),
            1.0, 0.0,
        )
        full = lax.dot_general(
            on, spread, (((0,), (0,)), ((), ())), preferred_element_type=jnp.float32
        )
        full = (full - 1.0) * 1e30
        for g in range(blocks):
            for p in range(4):
                bias[side, g, p] = full[g : g + 1, p * rows : (p + 1) * rows]

    mask_rows(0)
    got(2, 0)
    give(2, 0, 3, to_x)
    give(2, 0, 6, to_c)
    got(1, 1)
    give(1, 1, 3, to_y)
    give(1, 1, 5, to_c)
    got(1, 0)
    give(1, 0, 5, to_c)
    got(2, 1)
    give(2, 1, 6, to_c)
    for copy in tables:
        copy.wait_recv()
    mask_rows(1)

    def partial(mask, slots):
        zt = flip(z, mask, bits)
        best = None
        for n, r in enumerate(slots):
            pbr = flip(pb, (r // 2) % 2 * 2 + r // 4, 2)
            s = lax.dot_general(
                qq[mask, :, hd:], kv[r, :, 0:hd], NT, preferred_element_type=jnp.float32
            )
            s = jnp.concatenate(
                [
                    s[h * half : (h + 1) * half] + bias[r % 2, (zt * 2 + x) * 2 + h, pbr]
                    for h in range(2)
                ],
                axis=0,
            )
            s_scr[:, n * rows : (n + 1) * rows] = s
            top = jnp.maximum(s[:, :hd], s[:, hd:])
            best = top if best is None else jnp.maximum(best, top)
        peak = jnp.max(best, axis=1, keepdims=True)
        total = slope = None
        for n, r in enumerate(slots):
            p = jnp.exp2((s_scr[:, n * rows : (n + 1) * rows] - peak) * factor)
            t = lax.dot_general(
                qq[mask], kv[r, :, 0 : 2 * hd], NT, preferred_element_type=jnp.float32
            )
            pt = p * t
            p_scr[:, n * rows : (n + 1) * rows] = p.astype(jnp.bfloat16)
            ps_scr[:, n * rows : (n + 1) * rows] = pt.astype(jnp.bfloat16)
            p2 = p[:, :hd] + p[:, hd:]
            pt2 = pt[:, :hd] + pt[:, hd:]
            total = p2 if total is None else total + p2
            slope = pt2 if slope is None else slope + pt2
        total = jnp.sum(total, axis=1, keepdims=True)
        slope = jnp.sum(slope, axis=1, keepdims=True)
        lo, size = slots[0], len(slots)
        both = jnp.dot(
            p_scr[:, 0 : size * rows],
            kv[lo : lo + size, :, 2 * hd :].reshape(size * rows, 2 * hd),
            preferred_element_type=jnp.float32,
        )
        tang = jnp.dot(
            ps_scr[:, 0 : size * rows],
            kv[lo : lo + size, :, 2 * hd : 3 * hd].reshape(size * rows, hd),
            preferred_element_type=jnp.float32,
        )
        return peak, total, slope, both[:, :hd], tang * scale + both[:, hd:]

    def close(peak, total, slope, weighted, tang):
        mean = slope * scale / total
        centred = tang - mean * weighted
        lane = lax.broadcasted_iota(jnp.int32, (rows, hd), 1)
        stats = jnp.where(lane == 0, peak, jnp.where(lane == 1, total, mean))
        return weighted, centred, stats.T[0:8]

    def attend(mask):
        return close(*partial(mask, range(8)))

    def join(a, b):
        peak = jnp.maximum(a[0], b[0])
        fa, fb = jnp.exp2((a[0] - peak) * factor), jnp.exp2((b[0] - peak) * factor)
        return (peak,) + tuple(fa * m + fb * n for m, n in zip(a[1:], b[1:]))

    def result_copies(mask):
        dev = to_z(mask)
        return (
            remote(send.at[mask], recv.at[mask], rs.at[mask], rr.at[mask], dev),
            remote(sstat.at[mask], rstat.at[mask], ts.at[mask], tr.at[mask], dev),
        )

    def hand_in(mask, weighted, centred, stats):
        send[mask, :, 0:hd] = weighted.astype(jnp.bfloat16)
        send[mask, :, hd:] = centred.astype(jnp.bfloat16)
        sstat[mask] = stats
        for copy in result_copies(mask):
            copy.start()

    def got_queries(mask):
        remote(qq.at[0], qq.at[mask], qs.at[mask], qr.at[mask], to_c).wait_recv()

    far = zc - 1
    got_queries(far)
    for slot in (4, 5, 6):
        for h in range(2):
            got(slot, h)
    early = join(partial(far, (0, 1, 2)), partial(far, (4, 5, 6)))
    for h in range(2):
        got(3, h)
        give(3, h, 7, to_c)
    early = join(early, partial(far, (3,)))
    for h in range(2):
        got(7, h)
    hand_in(far, *close(*join(early, partial(far, (7,)))))

    def step(t, carry):
        mask = zc - 1 - t
        got_queries(mask)
        hand_in(mask, *attend(mask))
        return carry

    lax.fori_loop(1, zc - 1, step, 0)
    own_w, own_c, own_stats = attend(0)
    recv[0, :, 0:hd] = own_w.astype(jnp.bfloat16)
    recv[0, :, hd:] = own_c.astype(jnp.bfloat16)
    rstat[0] = own_stats
    for m in range(1, zc):
        for copy in result_copies(m):
            copy.wait_recv()

    peaks = [rstat[m, 0:1, :] for m in range(zc)]
    peak = functools.reduce(jnp.maximum, peaks)
    shares = [jnp.exp2((pk - peak) * factor) for pk in peaks]
    total = sum(a * rstat[m, 1:2, :] for m, a in enumerate(shares))
    mean = sum(a * rstat[m, 1:2, :] * rstat[m, 2:3, :] for m, a in enumerate(shares)) / total
    coef[...] = jnp.zeros_like(coef)
    for m, a in enumerate(shares):
        a = a / total
        coef[2 * m : 2 * m + 1, :] = a
        coef[2 * m + 1 : 2 * m + 2, :] = a * (rstat[m, 2:3, :] - mean)
    columns = coef[...].T
    out = outt = 0.0
    for m in range(zc):
        w = recv[m, :, 0:hd].astype(jnp.float32)
        d = recv[m, :, hd:].astype(jnp.float32)
        a, g = columns[:, 2 * m : 2 * m + 1], columns[:, 2 * m + 1 : 2 * m + 2]
        out = out + a * w
        outt = outt + (a * d + g * w)
    out_ref[:, 0:hd] = out.astype(out_ref.dtype)
    out_ref[:, hd:] = outt.astype(out_ref.dtype)
    for copy in sent:
        copy.wait_send()
    for copy in tables:
        copy.wait_send()
    for m in range(1, zc):
        for copy in result_copies(m):
            copy.wait_send()


def shards(
    queries, query_tangent, keys, values, key_tangent, value_tangent, block_list, block_count
):
    rows, hd = keys.shape
    slabs, pbs = lax.axis_size("kv"), lax.axis_size("pb")
    zc = slabs // 2
    list_t = block_list[:, 0, :].T
    count_t = block_count.T
    blocks = list_t.shape[1]
    vmem = pl.BlockSpec(memory_space=pltpu.VMEM)
    hbm = pl.BlockSpec(memory_space=pl.ANY)
    dma = pltpu.SemaphoreType.DMA
    out = pl.pallas_call(
        functools.partial(kernel, zc, slabs),
        out_shape=jax.ShapeDtypeStruct((rows, 2 * hd), jnp.bfloat16),
        in_specs=[hbm] * 8,
        out_specs=vmem,
        scratch_shapes=[
            pltpu.VMEM((8, rows, 4 * hd), jnp.bfloat16),
            pltpu.VMEM((zc, rows, 2 * hd), jnp.bfloat16),
            pltpu.VMEM((2,) + list_t.shape, jnp.int32),
            pltpu.VMEM((2, 1, blocks), jnp.int32),
            pltpu.VMEM((2, blocks, pbs, 1, rows), jnp.float32),
            pltpu.VMEM((rows, 8 * rows), jnp.float32),
            pltpu.VMEM((rows, 8 * rows), jnp.bfloat16),
            pltpu.VMEM((rows, 8 * rows), jnp.bfloat16),
            pltpu.VMEM((zc, rows, 2 * hd), jnp.bfloat16),
            pltpu.VMEM((zc, 8, rows), jnp.float32),
            pltpu.VMEM((zc, rows, 2 * hd), jnp.bfloat16),
            pltpu.VMEM((zc, 8, rows), jnp.float32),
            pltpu.VMEM((128, rows), jnp.float32),
            dma((8,)),
            dma((8, 2)),
            dma((8, 2)),
            dma((zc,)),
            dma((zc,)),
            dma((4,)),
            dma((zc,)),
            dma((zc,)),
            dma((zc,)),
            dma((zc,)),
        ],
        compiler_params=pltpu.CompilerParams(
            collective_id=0, has_side_effects=True, vmem_limit_bytes=62 * 1024 * 1024
        ),
    )(queries, query_tangent, keys, values, key_tangent, value_tangent, list_t, count_t)
    return out[:, :hd], out[:, hd:]


def solution(mesh):
    rows = P(("pb", "kv"), None)
    return jax.shard_map(
        shards,
        mesh=mesh,
        in_specs=(rows,) * 6 + (P("pb", "kv", None), P("pb", "kv")),
        out_specs=(rows, rows),
        check_vma=False,
    )
```

profile of v0, /device:TPU:0, one launch (start us, length us, event | category | flops | bytes accessed | tf_op | source)
XLA Modules:
  0.0 35.8 jit_solution(7035770142267516432)
XLA Ops:
  0.6 33.7 %shard_map.95 = bf16[256,256]{1,0:T(8,128)(2,1)} custom-call(bf16[256,128]{1,0:T(8,128)(2,1)} %q_in.1, bf16[256,128]{1,0:T(8,128)(2,1)} %qt_in.1, bf16[256,128]{1,0:T(8,128)(2,1)} %k_in.1, bf16[256,128]{1,0:T(8,128)(2,1)} %v_in.1, bf16[256,128]{1,0:T(8,128)(2,1)} %kt_in.1, bf16[256,128]{1,0:T(8,128)(2,1)} %vt_in.1, s32[8,16]{1,0:T(8,128)} %bitcast.4, ...), custom_call_target="tpu_custom_call" | custom-call | tf_op jit(solution)/shard_map/pallas_call | solution.py:292
  34.3 1.5 %fusion = (bf16[256,128]{1,0:T(8,128)(2,1)}, bf16[256,128]{1,0:T(8,128)(2,1)}) fusion(bf16[256,256]{1,0:T(8,128)(2,1)} %shard_map.95), kind=kLoop, calls=%fused_computation | loop fusion | bytes 262144 | tf_op jit(solution)/shard_map/slice | solution.py:326
where the time goes:
time: 36 us; the launch traced here: 35.8 us
  Pallas kernels  33.7 us (94%)
  local copies, waits for them, and re-layouts  1.53 us (4%)
  between operations  0.64 us (2%)
    pallas_call x1, Pallas kernels, shards(): pl.pallas_call(functools.partial(kernel, zc, slabs), out_shape=jax.ShapeD...  33.7 us
    slice x1, local copies, waits for them, and re-layouts, shards(): return (out[:, :hd], out[:, hd:])  1.53 us

commit v1 on v0

--- a/solution.py
+++ b/solution.py
@@ -24,7 +24,7 @@
 def kernel(
     zc, slabs, q_in, qt_in, k_in, v_in, kt_in, vt_in, list_in, count_in, out_ref,
     kv, qq, lst, cnt, bias, s_scr, p_scr, ps_scr, send, sstat, recv, rstat, coef,
-    local_sem, ks, kr, qs, qr, bs, rs, rr, ts, tr,
+    local_sem, ks, kr, qs, qr, qf, bs, rs, rr, ts, tr,
 ):
     rows, hd = q_in.shape
     half = rows // 2
@@ -33,6 +33,7 @@
     factor = scale * math.log2(math.e)
     pb, kvi = lax.axis_index("pb"), lax.axis_index("kv")
     y, c, z, x = pb // 2, pb % 2, kvi // 2, kvi % 2
+    inner = (z % 4 + 1) // 2 % 2
     to_x = (pb, kvi + 1 - 2 * x)
     to_y = (pb + 2 - 4 * y, kvi)
     to_c = (pb + 1 - 2 * c, kvi)
@@ -83,14 +84,30 @@
     def got(slot, h):
         remote(piece(slot, h), piece(slot, h), ks.at[slot, h], kr.at[slot, h], to_c).wait_recv()
 
+    def chunk(m, h):
+        return qq.at[m, pl.ds(h * half, half)]
+
+    def ask(m, slot, h, sem, dev):
+        return remote(chunk(m, h), chunk(slot, h), sem, qr.at[slot, h], dev)
+
+    def got_chunk(m, h):
+        ask(0, m, h, qs.at[m, h], to_c).wait_recv()
+
+    def pass_on(m, h):
+        @pl.when(inner == 1)
+        def _():
+            got_chunk(m, h)
+            ask(m, 5 - m, h, qf.at[m - 2, h], to_z(1)).start()
+
     give(0, 1, 1, to_x)
     give(0, 0, 2, to_y)
     give(0, 0, 1, to_x)
     give(0, 1, 2, to_y)
-    for m in range(zc - 1, 0, -1):
-        copy = remote(qq.at[0], qq.at[m], qs.at[m], qr.at[m], to_z(m))
-        copy.start()
-        sent.append(copy)
+    for m in [1 + 2 * inner, 2 - inner] + list(range(4, zc)):
+        for h in range(2):
+            copy = ask(0, m, h, qs.at[m, h], to_z(m))
+            copy.start()
+            sent.append(copy)
     give(0, 0, 4, to_c)
     give(0, 1, 4, to_c)
     tables = [
@@ -125,135 +142,181 @@
             for p in range(4):
                 bias[side, g, p] = full[g : g + 1, p * rows : (p + 1) * rows]
 
+    def partial(mask, pieces):
+        zt = flip(z, mask, bits)
+        best = None
+        at = 0
+        spans = []
+        for r, h in pieces:
+            pbr = flip(pb, (r // 2) % 2 * 2 + r // 4, 2)
+            lo, hi = (0, rows) if h is None else (h * half, h * half + half)
+            s = lax.dot_general(
+                qq[mask, :, hd:], kv[r, lo:hi, 0:hd], NT, preferred_element_type=jnp.float32
+            )
+            s = jnp.concatenate(
+                [
+                    s[g * half : (g + 1) * half]
+                    + bias[r % 2, (zt * 2 + x) * 2 + g, pbr][:, lo:hi]
+                    for g in range(2)
+                ],
+                axis=0,
+            )
+            s_scr[:, at : at + hi - lo] = s
+            for g in range(0, hi - lo, hd):
+                top = s[:, g : g + hd]
+                best = top if best is None else jnp.maximum(best, top)
+            spans.append((r, lo, hi, at))
+            at += hi - lo
+        peak = jnp.max(best, axis=1, keepdims=True)
+        total = slope = both = tang = None
+        for r, lo, hi, at in spans:
+            p = jnp.exp2((s_scr[:, at : at + hi - lo] - peak) * factor)
+            t = lax.dot_general(
+                qq[mask], kv[r, lo:hi, 0 : 2 * hd], NT, preferred_element_type=jnp.float32
+            )
+            pt = p * t
+            p_scr[:, at : at + hi - lo] = p.astype(jnp.bfloat16)
+            ps_scr[:, at : at + hi - lo] = pt.astype(jnp.bfloat16)
+            for g in range(0, hi - lo, hd):
+                p2, pt2 = p[:, g : g + hd], pt[:, g : g + hd]
+                total = p2 if total is None else total + p2
+                slope = pt2 if slope is None else slope + pt2
+        total = jnp.sum(total, axis=1, keepdims=True)
+        slope = jnp.sum(slope, axis=1, keepdims=True)
+        for r, lo, hi, at in spans:
+            a = jnp.dot(
+                p_scr[:, at : at + hi - lo], kv[r, lo:hi, 2 * hd :],
+                preferred_element_type=jnp.float32,
+            )
+            b = jnp.dot(
+                ps_scr[:, at : at + hi - lo], kv[r, lo:hi, 2 * hd : 3 * hd],
+                preferred_element_type=jnp.float32,
+            )
+            both = a if both is None else both + a
+            tang = b if tang is None else tang + b
+        return peak, total, slope, both[:, :hd], tang * scale + both[:, hd:]
+
+    def close(peak, total, slope, weighted, tang):
+        mean = slope * scale / total
+        centred = tang - mean * weighted
+        lane = lax.broadcasted_iota(jnp.int32, (rows, hd), 1)
+        stats = jnp.where(lane == 0, peak, jnp.where(lane == 1, total, mean))
+        return weighted, centred, stats.T[0:8]
+
+    def join(a, b):
+        peak = jnp.maximum(a[0], b[0])
+        fa, fb = jnp.exp2((a[0] - peak) * factor), jnp.exp2((b[0] - peak) * factor)
+        return (peak,) + tuple(fa * m + fb * n for m, n in zip(a[1:], b[1:]))
+
+    def result_copies(mask):
+        dev = to_z(1 + inner) if isinstance(mask, int) and mask == 2 else to_z(mask)
+        return (
+            remote(send.at[mask], recv.at[mask], rs.at[mask], rr.at[mask], dev),
+            remote(sstat.at[mask], rstat.at[mask], ts.at[mask], tr.at[mask], dev),
+        )
+
+    def hand_in(mask, weighted, centred, stats):
+        send[mask, :, 0:hd] = weighted.astype(jnp.bfloat16)
+        send[mask, :, hd:] = centred.astype(jnp.bfloat16)
+        sstat[mask] = stats
+        for copy in result_copies(mask):
+            copy.start()
+
+    def got_result(mask):
+        for copy in result_copies(mask):
+            copy.wait_recv()
+
+    def got_queries(mask):
+        for h in range(2):
+            got_chunk(mask, h)
+
+    most = tuple((r, None) for r in (0, 1, 2, 4, 5, 6))
+    last = ((3, None), (7, None))
+    whole = most + last
+
     mask_rows(0)
+    pass_on(3, 0)
     got(2, 0)
     give(2, 0, 3, to_x)
     give(2, 0, 6, to_c)
     got(1, 1)
     give(1, 1, 3, to_y)
     give(1, 1, 5, to_c)
+    pass_on(3, 1)
+    pass_on(2, 0)
     got(1, 0)
     give(1, 0, 5, to_c)
     got(2, 1)
     give(2, 1, 6, to_c)
+    pass_on(2, 1)
     for copy in tables:
         copy.wait_recv()
     mask_rows(1)
 
-    def partial(mask, slots):
-        zt = flip(z, mask, bits)
-        best = None
-        for n, r in enumerate(slots):
-            pbr = flip(pb, (r // 2) % 2 * 2 + r // 4, 2)
-            s = lax.dot_general(
-                qq[mask, :, hd:], kv[r, :, 0:hd], NT, preferred_element_type=jnp.float32
-            )
-            s = jnp.concatenate(
-                [
-                    s[h * half : (h + 1) * half] + bias[r % 2, (zt * 2 + x) * 2 + h, pbr]
-                    for h in range(2)
-                ],
-                axis=0,
-            )
-            s_scr[:, n * rows : (n + 1) * rows] = s
-            top = jnp.maximum(s[:, :hd], s[:, hd:])
-            best = top if best is None else jnp.maximum(best, top)
-        peak = jnp.max(best, axis=1, keepdims=True)
-        total = slope = None
-        for n, r in enumerate(slots):
-            p = jnp.exp2((s_scr[:, n * rows : (n + 1) * rows] - peak) * factor)
-            t = lax.dot_general(
-                qq[mask], kv[r, :, 0 : 2 * hd], NT, preferred_element_type=jnp.float32
-            )
-            pt = p * t
-            p_scr[:, n * rows : (n + 1) * rows] = p.astype(jnp.bfloat16)
-            ps_scr[:, n * rows : (n + 1) * rows] = pt.astype(jnp.bfloat16)
-            p2 = p[:, :hd] + p[:, hd:]
-            pt2 = pt[:, :hd] + pt[:, hd:]
-            total = p2 if total is None else total + p2
-            slope = pt2 if slope is None else slope + pt2
-        total = jnp.sum(total, axis=1, keepdims=True)
-        slope = jnp.sum(slope, axis=1, keepdims=True)
-        lo, size = slots[0], len(slots)
-        both = jnp.dot(
-            p_scr[:, 0 : size * rows],
-            kv[lo : lo + size, :, 2 * hd :].reshape(size * rows, 2 * hd),
-            preferred_element_type=jnp.float32,
-        )
-        tang = jnp.dot(
-            ps_scr[:, 0 : size * rows],
-            kv[lo : lo + size, :, 2 * hd : 3 * hd].reshape(size * rows, hd),
-            preferred_element_type=jnp.float32,
-        )
-        return peak, total, slope, both[:, :hd], tang * scale + both[:, hd:]
-
-    def close(peak, total, slope, weighted, tang):
-        mean = slope * scale / total
-        centred = tang - mean * weighted
-        lane = lax.broadcasted_iota(jnp.int32, (rows, hd), 1)
-        stats = jnp.where(lane == 0, peak, jnp.where(lane == 1, total, mean))
-        return weighted, centred, stats.T[0:8]
-
-    def attend(mask):
-        return close(*partial(mask, range(8)))
-
-    def join(a, b):
-        peak = jnp.maximum(a[0], b[0])
-        fa, fb = jnp.exp2((a[0] - peak) * factor), jnp.exp2((b[0] - peak) * factor)
-        return (peak,) + tuple(fa * m + fb * n for m, n in zip(a[1:], b[1:]))
-
-    def result_copies(mask):
-        dev = to_z(mask)
-        return (
-            remote(send.at[mask], recv.at[mask], rs.at[mask], rr.at[mask], dev),
-            remote(sstat.at[mask], rstat.at[mask], ts.at[mask], tr.at[mask], dev),
-        )
-
-    def hand_in(mask, weighted, centred, stats):
-        send[mask, :, 0:hd] = weighted.astype(jnp.bfloat16)
-        send[mask, :, hd:] = centred.astype(jnp.bfloat16)
-        sstat[mask] = stats
-        for copy in result_copies(mask):
-            copy.start()
-
-    def got_queries(mask):
-        remote(qq.at[0], qq.at[mask], qs.at[mask], qr.at[mask], to_c).wait_recv()
-
-    far = zc - 1
-    got_queries(far)
+    @pl.when(inner == 0)
+    def _():
+        got_queries(2)
+
     for slot in (4, 5, 6):
         for h in range(2):
             got(slot, h)
-    early = join(partial(far, (0, 1, 2)), partial(far, (4, 5, 6)))
+    second = partial(2, most)
     for h in range(2):
         got(3, h)
         give(3, h, 7, to_c)
-    early = join(early, partial(far, (3,)))
+
+    @pl.when(inner == 0)
+    def _():
+        got_queries(3)
+
     for h in range(2):
         got(7, h)
-    hand_in(far, *close(*join(early, partial(far, (7,)))))
-
-    def step(t, carry):
-        mask = zc - 1 - t
+    hand_in(2, *close(*join(second, partial(2, last))))
+    third = partial(3, whole)
+
+    @pl.when(inner == 0)
+    def _():
+        hand_in(3, *close(*third))
+
+    got_queries(1)
+    hand_in(1, *close(*partial(1, whole)))
+
+    def step(mask, carry):
         got_queries(mask)
-        hand_in(mask, *attend(mask))
+        hand_in(mask, *close(*partial(mask, whole)))
         return carry
 
-    lax.fori_loop(1, zc - 1, step, 0)
-    own_w, own_c, own_stats = attend(0)
+    if zc > 4:
+        lax.fori_loop(4, zc, step, 0)
+    own = partial(0, whole)
+    own_w, own_c, own_stats = close(*own)
     recv[0, :, 0:hd] = own_w.astype(jnp.bfloat16)
     recv[0, :, hd:] = own_c.astype(jnp.bfloat16)
     rstat[0] = own_stats
-    for m in range(1, zc):
-        for copy in result_copies(m):
-            copy.wait_recv()
+    coef[...] = jnp.zeros_like(coef)
+    got_result(2)
+
+    @pl.when(inner == 1)
+    def _():
+        coef[0:8, :] = rstat[2]
+        cols = coef[...].T
+        pk, tot, mean = cols[:, 0:1], cols[:, 1:2], cols[:, 2:3]
+        w = recv[2, :, 0:hd].astype(jnp.float32)
+        d = recv[2, :, hd:].astype(jnp.float32)
+        both = join(third, (pk, tot, mean * tot / scale, w, d + mean * w))
+        hand_in(3, *close(*both))
+        recv[2] = jnp.zeros_like(recv[2])
+        rstat[2] = jnp.concatenate([rstat[0, 0:1, :], jnp.zeros((7, rows), jnp.float32)], axis=0)
+        coef[0:8, :] = jnp.zeros((8, rows), jnp.float32)
+
+    for m in [1, 3] + list(range(4, zc)):
+        got_result(m)
 
     peaks = [rstat[m, 0:1, :] for m in range(zc)]
     peak = functools.reduce(jnp.maximum, peaks)
     shares = [jnp.exp2((pk - peak) * factor) for pk in peaks]
     total = sum(a * rstat[m, 1:2, :] for m, a in enumerate(shares))
     mean = sum(a * rstat[m, 1:2, :] * rstat[m, 2:3, :] for m, a in enumerate(shares)) / total
-    coef[...] = jnp.zeros_like(coef)
     for m, a in enumerate(shares):
         a = a / total
         coef[2 * m : 2 * m + 1, :] = a
@@ -270,6 +333,13 @@
     out_ref[:, hd:] = outt.astype(out_ref.dtype)
     for copy in sent:
         copy.wait_send()
+
+    @pl.when(inner == 1)
+    def _():
+        for m in (2, 3):
+            for h in range(2):
+                ask(m, 5 - m, h, qf.at[m - 2, h], to_z(1)).wait_send()
+
     for copy in tables:
         copy.wait_send()
     for m in range(1, zc):
@@ -311,8 +381,9 @@
             dma((8,)),
             dma((8, 2)),
             dma((8, 2)),
-            dma((zc,)),
-            dma((zc,)),
+            dma((zc, 2)),
+            dma((zc, 2)),
+            dma((2, 2)),
             dma((4,)),
             dma((zc,)),
             dma((zc,)),

time: 36 us -> 32.3 us (0.90)
  Pallas kernels: 33.7 us -> 30 us
    pallas_call x1, Pallas kernels: 33.7 us -> 30 us  [shards(): pl.pallas_call(functools.partial(kernel, zc, slabs), out_shape=jax.ShapeD...]
where the time goes in v1:
time: 32.3 us; the launch traced here: 32.2 us
  Pallas kernels  30 us (93%)
  local copies, waits for them, and re-layouts  1.53 us (5%)
  between operations  0.64 us (2%)
    pallas_call x1, Pallas kernels, shards(): pl.pallas_call(functools.partial(kernel, zc, slabs), out_shape=jax.ShapeD...  30 us
    slice x1, local copies, waits for them, and re-layouts, shards(): return (out[:, :hd], out[:, hd:])  1.53 us

profile of v1, /device:TPU:0, one launch (start us, length us, event | category | flops | bytes accessed | tf_op | source)
XLA Modules:
  0.0 32.2 jit_solution(5403530448657661604)
XLA Ops:
  0.6 30.0 %shard_map.95 = bf16[256,256]{1,0:T(8,128)(2,1)} custom-call(bf16[256,128]{1,0:T(8,128)(2,1)} %q_in.1, bf16[256,128]{1,0:T(8,128)(2,1)} %qt_in.1, bf16[256,128]{1,0:T(8,128)(2,1)} %k_in.1, bf16[256,128]{1,0:T(8,128)(2,1)} %v_in.1, bf16[256,128]{1,0:T(8,128)(2,1)} %kt_in.1, bf16[256,128]{1,0:T(8,128)(2,1)} %vt_in.1, s32[8,16]{1,0:T(8,128)} %bitcast.4, ...), custom_call_target="tpu_custom_call" | custom-call | tf_op jit(solution)/shard_map/pallas_call | solution.py:362
  30.6 1.5 %fusion = (bf16[256,128]{1,0:T(8,128)(2,1)}, bf16[256,128]{1,0:T(8,128)(2,1)}) fusion(bf16[256,256]{1,0:T(8,128)(2,1)} %shard_map.95), kind=kLoop, calls=%fused_computation | loop fusion | bytes 262144 | tf_op jit(solution)/shard_map/slice | solution.py:397

commit v2 on v1

--- a/solution.py
+++ b/solution.py
@@ -41,7 +41,9 @@
     def to_z(mask):
         return (pb, flip(z, mask, bits) * 2 + x)
 
-    loads = []
+    barrier = pltpu.get_barrier_semaphore()
+    for dev in [to_x, to_y, to_c] + [to_z(m) for m in range(1, zc)]:
+        pl.semaphore_signal(barrier, inc=1, device_id=dev, device_id_type=MESH)
     for n, (src, dst) in enumerate(
         [
             (k_in, kv.at[0, :, pl.ds(0, hd)]),
@@ -54,16 +56,11 @@
             (count_in, cnt.at[0]),
         ]
     ):
-        copy = pltpu.make_async_copy(src, dst, local_sem.at[n])
-        copy.start()
-        loads.append(copy)
-
-    barrier = pltpu.get_barrier_semaphore()
-    for dev in [to_x, to_y, to_c] + [to_z(m) for m in range(1, zc)]:
-        pl.semaphore_signal(barrier, inc=1, device_id=dev, device_id_type=MESH)
+        pltpu.make_async_copy(src, dst, local_sem.at[max(n // 4, n - 4)]).start()
+
     pl.semaphore_wait(barrier, 2 + zc)
-    for copy in loads:
-        copy.wait()
+    for n, ref in enumerate((kv.at[0], qq.at[0], lst.at[0], cnt.at[0])):
+        pltpu.make_async_copy(ref, ref, local_sem.at[n]).wait()
 
     def remote(src, dst, ssem, rsem, dev):
         return pltpu.make_async_remote_copy(
@@ -71,18 +68,15 @@
             device_id=dev, device_id_type=MESH,
         )
 
-    sent = []
-
     def piece(slot, h):
         return kv.at[slot, pl.ds(h * half, half)]
 
     def give(slot, h, dst, dev):
-        copy = remote(piece(slot, h), piece(dst, h), ks.at[dst, h], kr.at[dst, h], dev)
+        copy = remote(piece(slot, h), piece(dst, h), ks.at[0], kr.at[dst, h], dev)
         copy.start()
-        sent.append(copy)
 
     def got(slot, h):
-        remote(piece(slot, h), piece(slot, h), ks.at[slot, h], kr.at[slot, h], to_c).wait_recv()
+        remote(piece(slot, h), piece(slot, h), ks.at[0], kr.at[slot, h], to_c).wait_recv()
 
     def chunk(m, h):
         return qq.at[m, pl.ds(h * half, half)]
@@ -91,13 +85,13 @@
         return remote(chunk(m, h), chunk(slot, h), sem, qr.at[slot, h], dev)
 
     def got_chunk(m, h):
-        ask(0, m, h, qs.at[m, h], to_c).wait_recv()
+        ask(0, m, h, qs.at[0], to_c).wait_recv()
 
     def pass_on(m, h):
         @pl.when(inner == 1)
         def _():
             got_chunk(m, h)
-            ask(m, 5 - m, h, qf.at[m - 2, h], to_z(1)).start()
+            ask(m, 5 - m, h, qf.at[0], to_z(1)).start()
 
     give(0, 1, 1, to_x)
     give(0, 0, 2, to_y)
@@ -105,9 +99,8 @@
     give(0, 1, 2, to_y)
     for m in [1 + 2 * inner, 2 - inner] + list(range(4, zc)):
         for h in range(2):
-            copy = ask(0, m, h, qs.at[m, h], to_z(m))
+            copy = ask(0, m, h, qs.at[0], to_z(m))
             copy.start()
-            sent.append(copy)
     give(0, 0, 4, to_c)
     give(0, 1, 4, to_c)
     tables = [
@@ -211,8 +204,8 @@
     def result_copies(mask):
         dev = to_z(1 + inner) if isinstance(mask, int) and mask == 2 else to_z(mask)
         return (
-            remote(send.at[mask], recv.at[mask], rs.at[mask], rr.at[mask], dev),
-            remote(sstat.at[mask], rstat.at[mask], ts.at[mask], tr.at[mask], dev),
+            remote(send.at[mask], recv.at[mask], rs.at[0], rr.at[mask], dev),
+            remote(sstat.at[mask], rstat.at[mask], ts.at[0], tr.at[mask], dev),
         )
 
     def hand_in(mask, weighted, centred, stats):
@@ -331,20 +324,20 @@
         outt = outt + (a * d + g * w)
     out_ref[:, 0:hd] = out.astype(out_ref.dtype)
     out_ref[:, hd:] = outt.astype(out_ref.dtype)
-    for copy in sent:
-        copy.wait_send()
+    def all_sent(ref, sem):
+        remote(ref, ref, sem, sem, to_c).wait_send()
+
+    all_sent(kv.at[pl.ds(0, 7)], ks.at[0])
+    all_sent(qq.at[pl.ds(0, 2 + max(zc - 4, 0))], qs.at[0])
 
     @pl.when(inner == 1)
     def _():
-        for m in (2, 3):
-            for h in range(2):
-                ask(m, 5 - m, h, qf.at[m - 2, h], to_z(1)).wait_send()
+        all_sent(qq.at[pl.ds(0, 2)], qf.at[0])
 
     for copy in tables:
         copy.wait_send()
-    for m in range(1, zc):
-        for copy in result_copies(m):
-            copy.wait_send()
+    all_sent(send.at[pl.ds(1, zc - 1)], rs.at[0])
+    all_sent(sstat.at[pl.ds(1, zc - 1)], ts.at[0])
 
 
 def shards(
@@ -378,22 +371,22 @@
             pltpu.VMEM((zc, rows, 2 * hd), jnp.bfloat16),
             pltpu.VMEM((zc, 8, rows), jnp.float32),
             pltpu.VMEM((128, rows), jnp.float32),
-            dma((8,)),
+            dma((4,)),
+            dma((1,)),
             dma((8, 2)),
-            dma((8, 2)),
+            dma((1,)),
             dma((zc, 2)),
-            dma((zc, 2)),
-            dma((2, 2)),
+            dma((1,)),
             dma((4,)),
+            dma((1,)),
             dma((zc,)),
-            dma((zc,)),
-            dma((zc,)),
+            dma((1,)),
             dma((zc,)),
         ],
         compiler_params=pltpu.CompilerParams(
-            collective_id=0, has_side_effects=True, vmem_limit_bytes=62 * 1024 * 1024
+            collective_id=0, has_side_effects=True, vmem_limit_bytes=20 * 1024 * 1024
         ),
-    )(queries, query_tangent, keys, values, key_tangent, value_tangent, list_t, count_t)
+    )(*[pltpu.with_memory_space_constraint(a, pltpu.HBM) for a in (queries, query_tangent, keys, values, key_tangent, value_tangent, list_t, count_t)])
     return out[:, :hd], out[:, hd:]
 
 

time: 32.3 us -> 30.4 us (0.941)
  Pallas kernels: 30 us -> 29 us
  local copies, waits for them, and re-layouts: 1.53 us -> 0.66 us
    pallas_call x1, Pallas kernels: 30 us -> 29 us  [shards(): pl.pallas_call(functools.partial(kernel, zc, slabs), out_shape=jax.ShapeD...]
    slice x1, local copies, waits for them, and re-layouts: 1.53 us -> 0.66 us  [shards(): return (out[:, :hd], out[:, hd:])]
where the time goes in v2:
time: 30.4 us; the launch traced here: 30.3 us
  Pallas kernels  29 us (95%)
  local copies, waits for them, and re-layouts  0.66 us (2%)
  between operations  0.64 us (2%)
    pallas_call x1, Pallas kernels, shards(): pl.pallas_call(functools.partial(kernel, zc, slabs), out_shape=jax.ShapeD...  29 us
    slice x1, local copies, waits for them, and re-layouts, shards(): return (out[:, :hd], out[:, hd:])  0.66 us

profile of v2, /device:TPU:0, one launch (start us, length us, event | category | flops | bytes accessed | tf_op | source)
XLA Modules:
  0.0 30.3 jit_solution(17130074442483143346)
XLA Ops:
  0.6 29.0 %shard_map.95 = bf16[256,256]{1,0:T(8,128)(2,1)S(1)} custom-call(bf16[256,128]{1,0:T(8,128)(2,1)} %q_in.1, bf16[256,128]{1,0:T(8,128)(2,1)} %qt_in.1, bf16[256,128]{1,0:T(8,128)(2,1)} %k_in.1, bf16[256,128]{1,0:T(8,128)(2,1)} %v_in.1, bf16[256,128]{1,0:T(8,128)(2,1)} %kt_in.1, bf16[256,128]{1,0:T(8,128)(2,1)} %vt_in.1, s32[8,16]{1,0:T(8,128)} %bitcast.4, ...), custom_call_target="tpu_custom_call" | custom-call | tf_op jit(solution)/shard_map/pallas_call | solution.py:355
  29.6 0.7 %fusion = (bf16[256,128]{1,0:T(8,128)(2,1)}, bf16[256,128]{1,0:T(8,128)(2,1)}) fusion(bf16[256,256]{1,0:T(8,128)(2,1)S(1)} %shard_map.95), kind=kLoop, calls=%fused_computation | loop fusion | bytes 262144 | tf_op jit(solution)/shard_map/slice | solution.py:390

commit v3 on v2

--- a/solution.py
+++ b/solution.py
@@ -194,7 +194,8 @@
         centred = tang - mean * weighted
         lane = lax.broadcasted_iota(jnp.int32, (rows, hd), 1)
         stats = jnp.where(lane == 0, peak, jnp.where(lane == 1, total, mean))
-        return weighted, centred, stats.T[0:8]
+        flat = stats.T[0:4]
+        return weighted, centred, jnp.concatenate([flat[:, :half], flat[:, half:]], axis=0)
 
     def join(a, b):
         peak = jnp.maximum(a[0], b[0])
@@ -291,7 +292,7 @@
 
     @pl.when(inner == 1)
     def _():
-        coef[0:8, :] = rstat[2]
+        coef[0:4, :half], coef[0:4, half:] = rstat[2, 0:4], rstat[2, 4:8]
         cols = coef[...].T
         pk, tot, mean = cols[:, 0:1], cols[:, 1:2], cols[:, 2:3]
         w = recv[2, :, 0:hd].astype(jnp.float32)
@@ -299,21 +300,25 @@
         both = join(third, (pk, tot, mean * tot / scale, w, d + mean * w))
         hand_in(3, *close(*both))
         recv[2] = jnp.zeros_like(recv[2])
-        rstat[2] = jnp.concatenate([rstat[0, 0:1, :], jnp.zeros((7, rows), jnp.float32)], axis=0)
+        lane = lax.broadcasted_iota(jnp.int32, rstat.shape[1:], 0)
+        rstat[2] = jnp.where(lane % 4 == 0, rstat[0], 0.0)
         coef[0:8, :] = jnp.zeros((8, rows), jnp.float32)
 
     for m in [1, 3] + list(range(4, zc)):
         got_result(m)
 
-    peaks = [rstat[m, 0:1, :] for m in range(zc)]
+    def stat(m, n):
+        return jnp.concatenate([rstat[m, n : n + 1], rstat[m, n + 4 : n + 5]], axis=1)
+
+    peaks = [stat(m, 0) for m in range(zc)]
     peak = functools.reduce(jnp.maximum, peaks)
     shares = [jnp.exp2((pk - peak) * factor) for pk in peaks]
-    total = sum(a * rstat[m, 1:2, :] for m, a in enumerate(shares))
-    mean = sum(a * rstat[m, 1:2, :] * rstat[m, 2:3, :] for m, a in enumerate(shares)) / total
+    total = sum(a * stat(m, 1) for m, a in enumerate(shares))
+    mean = sum(a * stat(m, 1) * stat(m, 2) for m, a in enumerate(shares)) / total
     for m, a in enumerate(shares):
         a = a / total
         coef[2 * m : 2 * m + 1, :] = a
-        coef[2 * m + 1 : 2 * m + 2, :] = a * (rstat[m, 2:3, :] - mean)
+        coef[2 * m + 1 : 2 * m + 2, :] = a * (stat(m, 2) - mean)
     columns = coef[...].T
     out = outt = 0.0
     for m in range(zc):
@@ -367,9 +372,9 @@
             pltpu.VMEM((rows, 8 * rows), jnp.bfloat16),
             pltpu.VMEM((rows, 8 * rows), jnp.bfloat16),
             pltpu.VMEM((zc, rows, 2 * hd), jnp.bfloat16),
-            pltpu.VMEM((zc, 8, rows), jnp.float32),
+            pltpu.VMEM((zc, 8, rows // 2), jnp.float32),
             pltpu.VMEM((zc, rows, 2 * hd), jnp.bfloat16),
-            pltpu.VMEM((zc, 8, rows), jnp.float32),
+            pltpu.VMEM((zc, 8, rows // 2), jnp.float32),
             pltpu.VMEM((128, rows), jnp.float32),
             dma((4,)),
             dma((1,)),

time: 30.4 us -> 30.2 us (level)
  no operation moved by 1% of the time
where the time goes in v3:
time: 30.2 us; the launch traced here: 30.1 us
  Pallas kernels  28.8 us (95%)
  local copies, waits for them, and re-layouts  0.66 us (2%)
  between operations  0.64 us (2%)
    pallas_call x1, Pallas kernels, shards(): pl.pallas_call(functools.partial(kernel, zc, slabs), out_shape=jax.ShapeD...  28.8 us
    slice x1, local copies, waits for them, and re-layouts, shards(): return (out[:, :hd], out[:, hd:])  0.66 us

profile of v3, /device:TPU:0, one launch (start us, length us, event | category | flops | bytes accessed | tf_op | source)
XLA Modules:
  0.0 30.1 jit_solution(8459774709682250660)
XLA Ops:
  0.6 28.8 %shard_map.95 = bf16[256,256]{1,0:T(8,128)(2,1)S(1)} custom-call(bf16[256,128]{1,0:T(8,128)(2,1)} %q_in.1, bf16[256,128]{1,0:T(8,128)(2,1)} %qt_in.1, bf16[256,128]{1,0:T(8,128)(2,1)} %k_in.1, bf16[256,128]{1,0:T(8,128)(2,1)} %v_in.1, bf16[256,128]{1,0:T(8,128)(2,1)} %kt_in.1, bf16[256,128]{1,0:T(8,128)(2,1)} %vt_in.1, s32[8,16]{1,0:T(8,128)} %bitcast.4, ...), custom_call_target="tpu_custom_call" | custom-call | tf_op jit(solution)/shard_map/pallas_call | solution.py:360
  29.4 0.7 %fusion = (bf16[256,128]{1,0:T(8,128)(2,1)}, bf16[256,128]{1,0:T(8,128)(2,1)}) fusion(bf16[256,256]{1,0:T(8,128)(2,1)S(1)} %shard_map.95), kind=kLoop, calls=%fused_computation | loop fusion | bytes 262144 | tf_op jit(solution)/shard_map/slice | solution.py:395

commit v4 on v3

--- a/solution.py
+++ b/solution.py
@@ -192,33 +192,57 @@
     def close(peak, total, slope, weighted, tang):
         mean = slope * scale / total
         centred = tang - mean * weighted
-        lane = lax.broadcasted_iota(jnp.int32, (rows, hd), 1)
+        lane = lax.broadcasted_iota(jnp.int32, weighted.shape, 1)
         stats = jnp.where(lane == 0, peak, jnp.where(lane == 1, total, mean))
-        flat = stats.T[0:4]
-        return weighted, centred, jnp.concatenate([flat[:, :half], flat[:, half:]], axis=0)
+        return weighted, centred, stats.T[0:4]
+
+    def pack(flat, other=None):
+        other = flat[:, half:] if other is None else other
+        return jnp.concatenate([flat[:, :half], other], axis=0)
 
     def join(a, b):
         peak = jnp.maximum(a[0], b[0])
         fa, fb = jnp.exp2((a[0] - peak) * factor), jnp.exp2((b[0] - peak) * factor)
         return (peak,) + tuple(fa * m + fb * n for m, n in zip(a[1:], b[1:]))
 
+    low, high = slice(0, half), slice(half, rows)
+
     def result_copies(mask):
-        dev = to_z(1 + inner) if isinstance(mask, int) and mask == 2 else to_z(mask)
+        dev = to_z(1) if isinstance(mask, int) and mask == 2 else to_z(mask)
         return (
             remote(send.at[mask], recv.at[mask], rs.at[0], rr.at[mask], dev),
             remote(sstat.at[mask], rstat.at[mask], ts.at[0], tr.at[mask], dev),
         )
 
-    def hand_in(mask, weighted, centred, stats):
-        send[mask, :, 0:hd] = weighted.astype(jnp.bfloat16)
-        send[mask, :, hd:] = centred.astype(jnp.bfloat16)
-        sstat[mask] = stats
+    def put(slot, span, weighted, centred):
+        send[slot, span, 0:hd] = weighted.astype(jnp.bfloat16)
+        send[slot, span, hd:] = centred.astype(jnp.bfloat16)
+
+    def hand_in(mask, weighted, centred, flat):
+        put(mask, slice(None), weighted, centred)
+        sstat[mask] = pack(flat)
         for copy in result_copies(mask):
             copy.start()
 
-    def got_result(mask):
-        for copy in result_copies(mask):
-            copy.wait_recv()
+    def send_part(src, slot, span, stats, sem, dev):
+        remote(send.at[src, span], recv.at[slot, span], rs.at[0], rr.at[slot], dev).start()
+        if stats is not None:
+            remote(sstat.at[stats], rstat.at[slot], sem, tr.at[slot], dev).start()
+
+    def got_result(slot, span=slice(None)):
+        for ref, sem in ((recv.at[slot, span], rr), (rstat.at[slot], tr)):
+            remote(ref, ref, sem.at[slot], sem.at[slot], to_c).wait_recv()
+
+    def cut(part, span):
+        return tuple(a[span] for a in part)
+
+    def arrived(slot, span):
+        coef[0:4, :half], coef[0:4, half:] = rstat[slot, 0:4], rstat[slot, 4:8]
+        cols = coef[:, span].T
+        pk, tot, mean = cols[:, 0:1], cols[:, 1:2], cols[:, 2:3]
+        w = recv[slot, span, 0:hd].astype(jnp.float32)
+        d = recv[slot, span, hd:].astype(jnp.float32)
+        return pk, tot, mean * tot / scale, w, d + mean * w
 
     def got_queries(mask):
         for h in range(2):
@@ -259,21 +283,57 @@
         got(3, h)
         give(3, h, 7, to_c)
 
-    @pl.when(inner == 0)
-    def _():
-        got_queries(3)
-
     for h in range(2):
         got(7, h)
-    hand_in(2, *close(*join(second, partial(2, last))))
-    third = partial(3, whole)
-
-    @pl.when(inner == 0)
-    def _():
-        hand_in(3, *close(*third))
-
-    got_queries(1)
-    hand_in(1, *close(*partial(1, whole)))
+    coef[...] = jnp.zeros_like(coef)
+    second = close(*join(second, partial(2, last)))
+
+    @pl.when(inner == 0)
+    def _():
+        hand_in(2, *second)
+
+    line = lax.broadcasted_iota(jnp.int32, (8, half), 0)
+
+    @pl.when(inner == 1)
+    def _():
+        put(2, slice(None), *second[:2])
+        stats = pack(second[2])
+        sstat[zc] = stats
+        sstat[2] = jnp.where((line < 4) | (line % 4 == 0), stats, 0.0)
+        send_part(2, zc, high, zc, ts.at[1], to_z(3))
+        send_part(2, 2, low, 2, ts.at[0], to_z(2))
+
+    soon, later = 3 - 2 * inner, 1 + 2 * inner
+    got_queries(soon)
+    first = partial(soon, whole)
+    near = close(*first)
+
+    @pl.when(inner == 0)
+    def _():
+        hand_in(3, *near)
+
+    @pl.when(inner == 1)
+    def _():
+        put(1, low, *cut(near[:2], low))
+        send_part(1, 1, low, None, None, to_z(1))
+
+    @pl.when(inner == 0)
+    def _():
+        got_queries(1)
+
+    third = partial(later, whole)
+
+    @pl.when(inner == 0)
+    def _():
+        hand_in(1, *close(*third))
+
+    @pl.when(inner == 1)
+    def _():
+        got_result(zc, high)
+        w, centred, flat = close(*join(cut(first, high), arrived(zc, high)))
+        put(1, high, w, centred)
+        sstat[1] = pack(near[2], flat)
+        send_part(1, 1, high, 1, ts.at[0], to_z(1))
 
     def step(mask, carry):
         got_queries(mask)
@@ -283,26 +343,23 @@
     if zc > 4:
         lax.fori_loop(4, zc, step, 0)
     own = partial(0, whole)
-    own_w, own_c, own_stats = close(*own)
+    own_w, own_c, own_flat = close(*own)
     recv[0, :, 0:hd] = own_w.astype(jnp.bfloat16)
     recv[0, :, hd:] = own_c.astype(jnp.bfloat16)
-    rstat[0] = own_stats
-    coef[...] = jnp.zeros_like(coef)
-    got_result(2)
-
-    @pl.when(inner == 1)
-    def _():
-        coef[0:4, :half], coef[0:4, half:] = rstat[2, 0:4], rstat[2, 4:8]
-        cols = coef[...].T
-        pk, tot, mean = cols[:, 0:1], cols[:, 1:2], cols[:, 2:3]
-        w = recv[2, :, 0:hd].astype(jnp.float32)
-        d = recv[2, :, hd:].astype(jnp.float32)
-        both = join(third, (pk, tot, mean * tot / scale, w, d + mean * w))
-        hand_in(3, *close(*both))
+    rstat[0] = pack(own_flat)
+
+    @pl.when(inner == 1)
+    def _():
+        got_result(2)
+        hand_in(3, *close(*join(third, arrived(2, slice(None)))))
         recv[2] = jnp.zeros_like(recv[2])
-        lane = lax.broadcasted_iota(jnp.int32, rstat.shape[1:], 0)
-        rstat[2] = jnp.where(lane % 4 == 0, rstat[0], 0.0)
+        rstat[2] = jnp.where(line % 4 == 0, rstat[0], 0.0)
         coef[0:8, :] = jnp.zeros((8, rows), jnp.float32)
+
+    @pl.when(inner == 0)
+    def _():
+        got_result(2, low)
+        recv[2, half:] = jnp.zeros((half, 2 * hd), jnp.bfloat16)
 
     for m in [1, 3] + list(range(4, zc)):
         got_result(m)
@@ -343,6 +400,10 @@
         copy.wait_send()
     all_sent(send.at[pl.ds(1, zc - 1)], rs.at[0])
     all_sent(sstat.at[pl.ds(1, zc - 1)], ts.at[0])
+
+    @pl.when(inner == 1)
+    def _():
+        all_sent(sstat.at[0], ts.at[1])
 
 
 def shards(
@@ -372,9 +433,9 @@
             pltpu.VMEM((rows, 8 * rows), jnp.bfloat16),
             pltpu.VMEM((rows, 8 * rows), jnp.bfloat16),
             pltpu.VMEM((zc, rows, 2 * hd), jnp.bfloat16),
-            pltpu.VMEM((zc, 8, rows // 2), jnp.float32),
-            pltpu.VMEM((zc, rows, 2 * hd), jnp.bfloat16),
-            pltpu.VMEM((zc, 8, rows // 2), jnp.float32),
+            pltpu.VMEM((zc + 1, 8, rows // 2), jnp.float32),
+            pltpu.VMEM((zc + 1, rows, 2 * hd), jnp.bfloat16),
+            pltpu.VMEM((zc + 1, 8, rows // 2), jnp.float32),
             pltpu.VMEM((128, rows), jnp.float32),
             dma((4,)),
             dma((1,)),
@@ -384,9 +445,9 @@
             dma((1,)),
             dma((4,)),
             dma((1,)),
-            dma((zc,)),
-            dma((1,)),
-            dma((zc,)),
+            dma((zc + 1,)),
+            dma((2,)),
+            dma((zc + 1,)),
         ],
         compiler_params=pltpu.CompilerParams(
             collective_id=0, has_side_effects=True, vmem_limit_bytes=20 * 1024 * 1024

time: 30.2 us -> 29.8 us (0.987)
  Pallas kernels: 28.8 us -> 28.3 us
    pallas_call x1, Pallas kernels: 28.8 us -> 28.3 us  [shards(): pl.pallas_call(functools.partial(kernel, zc, slabs), out_shape=jax.ShapeD...]
where the time goes in v4:
time: 29.8 us; the launch traced here: 29.6 us
  Pallas kernels  28.3 us (95%)
  local copies, waits for them, and re-layouts  0.66 us (2%)
  between operations  0.64 us (2%)
    pallas_call x1, Pallas kernels, shards(): pl.pallas_call(functools.partial(kernel, zc, slabs), out_shape=jax.ShapeD...  28.3 us
    slice x1, local copies, waits for them, and re-layouts, shards(): return (out[:, :hd], out[:, hd:])  0.66 us

profile of v4, /device:TPU:0, one launch (start us, length us, event | category | flops | bytes accessed | tf_op | source)
XLA Modules:
  0.0 29.6 jit_solution(14872332040196463337)
XLA Ops:
  0.6 28.3 %shard_map.95 = bf16[256,256]{1,0:T(8,128)(2,1)S(1)} custom-call(bf16[256,128]{1,0:T(8,128)(2,1)} %q_in.1, bf16[256,128]{1,0:T(8,128)(2,1)} %qt_in.1, bf16[256,128]{1,0:T(8,128)(2,1)} %k_in.1, bf16[256,128]{1,0:T(8,128)(2,1)} %v_in.1, bf16[256,128]{1,0:T(8,128)(2,1)} %kt_in.1, bf16[256,128]{1,0:T(8,128)(2,1)} %vt_in.1, s32[8,16]{1,0:T(8,128)} %bitcast.4, ...), custom_call_target="tpu_custom_call" | custom-call | tf_op jit(solution)/shard_map/pallas_call | solution.py:421
  29.0 0.7 %fusion = (bf16[256,128]{1,0:T(8,128)(2,1)}, bf16[256,128]{1,0:T(8,128)(2,1)}) fusion(bf16[256,256]{1,0:T(8,128)(2,1)S(1)} %shard_map.95), kind=kLoop, calls=%fused_computation | loop fusion | bytes 262144 | tf_op jit(solution)/shard_map/slice | solution.py:456
